TPU v7x, 512 devices: a whole 4x8x8 slice. The times are simulated.
512 devices in a mesh: term: 8 (over z), sector: 64 (over x, y, core).
Axes of the slice: x: 4, y: 8, z: 8, core: 2. Of those that a mesh axis runs over, the one named last changes fastest.
Arguments:
- wave_tiles: bfloat16 [1024, 2, 128, 128], P('sector'), may hold values from -6 to 6
- left_env: bfloat16 [8, 64, 128, 128], P('term', 'sector'), may hold values from -0.5 to 0.5
- right_env: bfloat16 [8, 64, 128, 128], P('term', 'sector'), may hold values from -0.5 to 0.5
- send_list: int32 [64, 128], P('sector'), may hold values from -1 to 15, as said below
- left_tasks: int32 [8, 64, 96, 3], P('term', 'sector'), may hold values from 0 to 127, as said below
- right_tasks: int32 [8, 64, 256, 3], P('term', 'sector'), may hold values from 0 to 63, as said below
Outputs:
- sigma: float32 [1024, 2, 128, 128], P('sector', None, 'term')
Inputs may be any that keep to these rules, and one draw needn't show every extreme that they name: send_list[s, o * 2 + c] is a tile index local to sender s, or -1 for an empty slot; some owner drawn from the seed receives a full 2 tiles from every sender. `left_tasks`: entries 0, 1, 2 lie below 64, 128 and 32. `right_tasks`: entries 0, 1, 2 lie below 32, 64 and 16.
All inputs are finite; a program needn't handle non-finite values.
Results may differ from a plain program's by a relative error of at most 0.0029.
Values may be sent and summed in bfloat16 or wider, within the bound.
A program may use at most 128 MiB of HBM per device.

v0:
```python
import math
import jax
import jax.numpy as jnp
from jax import lax
from jax.sharding import PartitionSpec as P

INTER_TILES = 32


def run_tasks(tasks, first_tiles, second_tiles, contract, count):
    block = math.gcd(tasks.shape[0], 32)
    shape = (count,) + tuple(contract(first_tiles[:1], second_tiles[:1]).shape[1:])

    def step(turn, total):
        rows = lax.dynamic_slice_in_dim(tasks, turn * block, block, 0)
        first = jnp.take(first_tiles, rows[:, 0], axis=0)
        second = jnp.take(second_tiles, rows[:, 1], axis=0)
        return total.at[rows[:, 2]].add(contract(first, second))

    return lax.fori_loop(0, tasks.shape[0] // block, step, jnp.zeros(shape, jnp.float32))


def left_product(env_part, wave_part):
    return jnp.einsum("bij,bvjk->bvik", env_part, wave_part, preferred_element_type=jnp.float32)


def right_product(inter_part, env_part):
    return jnp.einsum("bvij,bjk->bvik", inter_part, env_part, preferred_element_type=jnp.float32)


def shards(wave_tiles, left_env, right_env, send_list, left_tasks, right_tasks):
    env_left, env_right = (
        lax.all_gather(left_env, "sector", axis=1, tiled=True),
        lax.all_gather(right_env, "sector", axis=1, tiled=True),
    )
    env_left = env_left[0]
    env_right = env_right[0]
    slot_list = send_list[0]
    live = slot_list >= 0
    picked = jnp.take(wave_tiles, jnp.maximum(slot_list, 0), axis=0)
    outgoing = jnp.where(live[:, None, None, None], picked, jnp.zeros((), jnp.bfloat16))
    tile_dim = wave_tiles.shape[2]
    groups = lax.axis_size("term")
    share = tile_dim // groups
    received = lax.all_to_all(outgoing, "sector", split_axis=0, concat_axis=0, tiled=True)
    inter = run_tasks(left_tasks[0, 0], env_left, received, left_product, INTER_TILES).astype(
        jnp.bfloat16
    )
    partial_value = run_tasks(
        right_tasks[0, 0], inter, env_right, right_product, wave_tiles.shape[0]
    )
    summed = lax.psum(partial_value, "term")
    return lax.dynamic_slice_in_dim(summed, lax.axis_index("term") * share, share, 2)


def solution(mesh):
    in_specs = (
        P("sector", None, None, None),
        P("term", "sector", None, None),
        P("term", "sector", None, None),
        P("sector", None),
        P("term", "sector", None, None),
        P("term", "sector", None, None),
    )
    out_specs = P("sector", None, "term", None)
    return jax.shard_map(shards, mesh=mesh, in_specs=in_specs, out_specs=out_specs, check_vma=False)
```

profile of v0, /device:TPU:2, one launch (start us, length us, event | category | flops | bytes accessed | tf_op | source)
XLA Modules:
  0.0 562.8 jit_solution(14975568767976974510)
XLA Ops:
  8.0 6.5 %gather_fusion.4 = bf16[128,2,128,128]{3,2,1,0:T(8,128)(2,1)} fusion(bf16[16,2,128,128]{3,2,1,0:T(8,128)(2,1)S(1)} %copy-done, s32[1024]{0:T(1024)S(1)} %pad_clamp_fusion.4), kind=kCustom, calls=%fused_computation.4 | custom fusion | bytes 16777728 | tf_op jit(solution)/shard_map/jit(_take)/gather | solution.py:40
  14.5 7.5 %select_select_fusion = bf16[128,2,128,128]{3,2,1,0:T(8,128)(2,1)} fusion(bf16[128,2,128,128]{3,2,1,0:T(8,128)(2,1)} %gather_fusion.4, pred[128]{0:T(512)(128)(4,1)S(1)} %get-tuple-element.225, pred[128]{0:T(512)(128)(4,1)S(1)} %get-tuple-element.224), kind=kLoop, calls=%fused_computation.45 | loop fusion | flops 8388608 | bytes 16777472 | tf_op jit(solution)/shard_map/jit(_where)/select_n | solution.py:41
  22.0 11.3 %all-to-all-start = ((bf16[128,2,128,128]{3,2,1,0:T(8,128)(2,1)}), bf16[128,2,128,128]{3,2,1,0:T(8,128)(2,1)}, u32[]{:S(2)}, u32[]{:S(2)}) async-start(bf16[128,2,128,128]{3,2,1,0:T(8,128)(2,1)} %select_select_fusion), calls=%async_computation | async-start | bytes 16777216 | tf_op jit(solution)/shard_map/all_to_all | solution.py:45
  34.8 102.3 %all-gather.3.cloned.1.call-done = bf16[1,64,128,128]{3,2,0,1:T(8,128)(2,1)} async-done(((bf16[1,1,128,128]{3,2,0,1:T(8,128)(2,1)}), bf16[1,64,128,128]{3,2,0,1:T(8,128)(2,1)}) %all-gather.3.cloned.1.call-update) | async-done | bytes 2097168 | tf_op jit(solution)/shard_map/all_gather | solution.py:33
  137.1 90.6 %all-to-all-done = bf16[128,2,128,128]{3,2,1,0:T(8,128)(2,1)} async-done(((bf16[128,2,128,128]{3,2,1,0:T(8,128)(2,1)}), bf16[128,2,128,128]{3,2,1,0:T(8,128)(2,1)}, u32[]{:S(2)}, u32[]{:S(2)}) %all-to-all-start) | async-done | bytes 8388640 | tf_op jit(solution)/shard_map/all_to_all | solution.py:45
  230.2 82.3 %while.26 = (s32[]{:T(128)}, f32[32,2,128,128]{3,2,1,0:T(8,128)}, s32[96,3]{0,1:T(4,128)S(1)}, bf16[128,2,128,128]{3,2,1,0:T(8,128)(2,1)}, bf16[64,128,128]{2,1,...) while((s32[]{:T(128)}, f32[32,2,128,128]{3,2,1,0:T(8,128)}, s32[96,3]{0,1:T(4,128)S(1)}, ...), condition=%wide.region_2.4_spmd, body=%wide.region_0.3_spmd.sunk | while | flops 271059520 | bytes 34613776 | solution.py:20
  242.1 5.6 copy.23
  247.7 10.1 %scatter_fusion = f32[32,2,128,128]{3,2,1,0:T(8,128)} fusion(f32[32,2,128,128]{3,2,1,0:T(8,128)} %get-tuple-element.314, s32[32]{0:T(128)S(1)} %get-tuple-element.291, f32[32,2,128,128]{3,2,1,0:T(8,128)} %copy.23), kind=kCustom, calls=%fused_computation.5.clone.1 | custom fusion | flops 1048576 | bytes 12583040 | tf_op jit(solution)/shard_map/while/body/eval_jaxpr/scatter-add | solution.py:18
  269.6 5.6 copy.23
  275.2 9.9 %scatter_fusion = f32[32,2,128,128]{3,2,1,0:T(8,128)} fusion(f32[32,2,128,128]{3,2,1,0:T(8,128)} %get-tuple-element.314, s32[32]{0:T(128)S(1)} %get-tuple-element.291, f32[32,2,128,128]{3,2,1,0:T(8,128)} %copy.23), kind=kCustom, calls=%fused_computation.5.clone.1 | custom fusion | flops 1048576 | bytes 12583040 | tf_op jit(solution)/shard_map/while/body/eval_jaxpr/scatter-add | solution.py:18
  296.9 5.6 copy.23
  302.6 9.9 %scatter_fusion = f32[32,2,128,128]{3,2,1,0:T(8,128)} fusion(f32[32,2,128,128]{3,2,1,0:T(8,128)} %get-tuple-element.314, s32[32]{0:T(128)S(1)} %get-tuple-element.291, f32[32,2,128,128]{3,2,1,0:T(8,128)} %copy.23), kind=kCustom, calls=%fused_computation.5.clone.1 | custom fusion | flops 1048576 | bytes 12583040 | tf_op jit(solution)/shard_map/while/body/eval_jaxpr/scatter-add | solution.py:18
  316.6 145.3 %while.27 = (s32[]{:T(128)}, f32[16,2,128,128]{3,2,1,0:T(8,128)S(1)}, s32[256,3]{0,1:T(4,128)S(1)}, bf16[32,2,128,128]{3,2,1,0:T(8,128)(2,1)}, bf16[64,128,128]{...) while((s32[]{:T(128)}, f32[16,2,128,128]{3,2,1,0:T(8,128)S(1)}, ...), condition=%wide.region_5.7_spmd, body=%wide.region_3.6_spmd.sunk | while | flops 271059520 | bytes 26225168 | solution.py:20
  323.7 4.6 fusion.34
  328.3 6.5 %scatter_fusion.1 = f32[16,2,128,128]{3,2,1,0:T(8,128)S(1)} fusion(f32[16,2,128,128]{3,2,1,0:T(8,128)S(1)} %get-tuple-element.341, s32[32]{0:T(128)S(1)} %get-tuple-element.300, f32[32,2,128,128]{3,2,1,0:T(8,128)} %fusion.34), kind=kCustom, calls=%fused_computation.6.clone.1 | custom fusion | flops 1048576 | bytes 12583040 | tf_op jit(solution)/shard_map/while/body/eval_jaxpr/scatter-add | solution.py:18
  346.5 6.5 %scatter_fusion.1 = f32[16,2,128,128]{3,2,1,0:T(8,128)S(1)} fusion(f32[16,2,128,128]{3,2,1,0:T(8,128)S(1)} %get-tuple-element.341, s32[32]{0:T(128)S(1)} %get-tuple-element.300, f32[32,2,128,128]{3,2,1,0:T(8,128)} %fusion.34), kind=kCustom, calls=%fused_computation.6.clone.1 | custom fusion | flops 1048576 | bytes 12583040 | tf_op jit(solution)/shard_map/while/body/eval_jaxpr/scatter-add | solution.py:18
  364.6 6.5 %scatter_fusion.1 = f32[16,2,128,128]{3,2,1,0:T(8,128)S(1)} fusion(f32[16,2,128,128]{3,2,1,0:T(8,128)S(1)} %get-tuple-element.341, s32[32]{0:T(128)S(1)} %get-tuple-element.300, f32[32,2,128,128]{3,2,1,0:T(8,128)} %fusion.34), kind=kCustom, calls=%fused_computation.6.clone.1 | custom fusion | flops 1048576 | bytes 12583040 | tf_op jit(solution)/shard_map/while/body/eval_jaxpr/scatter-add | solution.py:18
  382.8 6.5 %scatter_fusion.1 = f32[16,2,128,128]{3,2,1,0:T(8,128)S(1)} fusion(f32[16,2,128,128]{3,2,1,0:T(8,128)S(1)} %get-tuple-element.341, s32[32]{0:T(128)S(1)} %get-tuple-element.300, f32[32,2,128,128]{3,2,1,0:T(8,128)} %fusion.34), kind=kCustom, calls=%fused_computation.6.clone.1 | custom fusion | flops 1048576 | bytes 12583040 | tf_op jit(solution)/shard_map/while/body/eval_jaxpr/scatter-add | solution.py:18
  400.9 6.5 %scatter_fusion.1 = f32[16,2,128,128]{3,2,1,0:T(8,128)S(1)} fusion(f32[16,2,128,128]{3,2,1,0:T(8,128)S(1)} %get-tuple-element.341, s32[32]{0:T(128)S(1)} %get-tuple-element.300, f32[32,2,128,128]{3,2,1,0:T(8,128)} %fusion.34), kind=kCustom, calls=%fused_computation.6.clone.1 | custom fusion | flops 1048576 | bytes 12583040 | tf_op jit(solution)/shard_map/while/body/eval_jaxpr/scatter-add | solution.py:18
  419.1 6.5 %scatter_fusion.1 = f32[16,2,128,128]{3,2,1,0:T(8,128)S(1)} fusion(f32[16,2,128,128]{3,2,1,0:T(8,128)S(1)} %get-tuple-element.341, s32[32]{0:T(128)S(1)} %get-tuple-element.300, f32[32,2,128,128]{3,2,1,0:T(8,128)} %fusion.34), kind=kCustom, calls=%fused_computation.6.clone.1 | custom fusion | flops 1048576 | bytes 12583040 | tf_op jit(solution)/shard_map/while/body/eval_jaxpr/scatter-add | solution.py:18
  432.7 4.6 fusion.34
  437.2 6.5 %scatter_fusion.1 = f32[16,2,128,128]{3,2,1,0:T(8,128)S(1)} fusion(f32[16,2,128,128]{3,2,1,0:T(8,128)S(1)} %get-tuple-element.341, s32[32]{0:T(128)S(1)} %get-tuple-element.300, f32[32,2,128,128]{3,2,1,0:T(8,128)} %fusion.34), kind=kCustom, calls=%fused_computation.6.clone.1 | custom fusion | flops 1048576 | bytes 12583040 | tf_op jit(solution)/shard_map/while/body/eval_jaxpr/scatter-add | solution.py:18
  455.4 6.5 %scatter_fusion.1 = f32[16,2,128,128]{3,2,1,0:T(8,128)S(1)} fusion(f32[16,2,128,128]{3,2,1,0:T(8,128)S(1)} %get-tuple-element.341, s32[32]{0:T(128)S(1)} %get-tuple-element.300, f32[32,2,128,128]{3,2,1,0:T(8,128)} %fusion.34), kind=kCustom, calls=%fused_computation.6.clone.1 | custom fusion | flops 1048576 | bytes 12583040 | tf_op jit(solution)/shard_map/while/body/eval_jaxpr/scatter-add | solution.py:18
  463.2 91.4 %all-reduce.2.cloned.1.call-done = f32[16,2,128,128]{3,2,1,0:T(8,128)} async-done(((f32[16,2,128,128]{3,2,1,0:T(8,128)}), f32[16,2,128,128]{3,2,1,0:T(8,128)}) %all-reduce.2.cloned.1.call-update) | async-done | bytes 2097168 | tf_op jit(solution)/shard_map/psum | solution.py:52
  (121 shorter events, 131.9 us)
Async XLA Ops:
  6.5 1.4 copy-start
  22.0 12.8 %copy-start.3 = (s32[1,1,96,3]{2,1,3,0:T(1,128)S(1)}, s32[1,1,96,3]{2,1,3,0:T(1,128)}, u32[]{:S(2)}) copy-start(s32[1,1,96,3]{2,1,3,0:T(1,128)} %param.16) | copy-start | bytes 3460
  22.0 12.8 %copy-start.2 = (s32[1,1,256,3]{2,1,3,0:T(1,128)S(1)}, s32[1,1,256,3]{2,1,3,0:T(1,128)}, u32[]{:S(2)}) copy-start(s32[1,1,256,3]{2,1,3,0:T(1,128)} %param.17) | copy-start | bytes 9220
  22.0 205.8 %all-to-all-start = ((bf16[128,2,128,128]{3,2,1,0:T(8,128)(2,1)}), bf16[128,2,128,128]{3,2,1,0:T(8,128)(2,1)}, u32[]{:S(2)}, u32[]{:S(2)}) async-start(bf16[128,2,128,128]{3,2,1,0:T(8,128)(2,1)} %select_select_fusion), calls=%async_computation | async-start | bytes 16777216 | tf_op jit(solution)/shard_map/all_to_all | solution.py:45
  33.3 103.9 %all-gather.3.cloned.1.call-start = ((), (), s32[]{:S(2)}) async-start(), calls=%async_computation.1 | async-start | bytes 2129920 | tf_op jit(solution)/shard_map/all_gather | solution.py:33
  34.0 282.4 %all-gather.5.cloned.1.call-start = ((), (), s32[]{:S(2)}) async-start(), calls=%async_computation.2 | async-start | bytes 2129920 | tf_op jit(solution)/shard_map/all_gather | solution.py:34
  34.8 519.8 %all-reduce.2.cloned.1.call-start = ((), (), s32[]{:S(2)}) async-start(), calls=%async_computation.3 | async-start | bytes 4194304 | tf_op jit(solution)/shard_map/psum | solution.py:52
  461.9 1.3 copy-start.1
Sparse Core Ops, SparseCore 0:
  37.5 99.6 all-gather.2
  140.5 95.8 all-gather.4
  463.3 91.2 all-reduce.1
where the time goes:
time: 565 us; the launch traced here: 563 us
  waiting for transfers between devices  286 us (51%)
  local copies, waits for them, and re-layouts  109 us (19%)
  other arithmetic  95 us (17%)
  matrix products  48.7 us (9%)
  between operations  13.2 us (2%)
  starting transfers between devices  11.4 us (2%)
    all_gather x1, waiting for transfers between devices, shards(): lax.all_gather(left_env, 'sector', axis=1, tiled=True)  102 us
    psum x1, waiting for transfers between devices, shards(): summed = lax.psum(partial_value, 'term')  91.4 us
    all_to_all x1, waiting for transfers between devices, shards(): lax.all_to_all(outgoing, 'sector', split_axis=0, concat_axis=0, tiled=True)  90.6 us
    scatter-add x11, other arithmetic, step(): return total.at[rows[:, 2]].add(contract(first, second))  81.8 us
    gather x11, local copies, waits for them, and re-layouts, step(): first = jnp.take(first_tiles, rows[:, 0], axis=0)  39.8 us
    gather x11, local copies, waits for them, and re-layouts, step(): second = jnp.take(second_tiles, rows[:, 1], axis=0)  38.9 us
    dot_general x8, matrix products, right_product(): jnp.einsum('bvij,bjk->bvik', inter_part, env_part, preferred_element_type...  36.6 us
    transpose x3, local copies, waits for them, and re-layouts, left_product(): jnp.einsum('bij,bvjk->bvik', env_part, wave_part, preferred_element_type=...  16.9 us
  transfers between devices with their start and end apart: 4, of which 3 were waited for; matrix products, arithmetic and copies ran while one was open for 16% of the time, Pallas kernels for 0%

commit v1 on v0

--- a/solution.py
+++ b/solution.py
@@ -5,6 +5,14 @@
 from jax.sharding import PartitionSpec as P
 
 INTER_TILES = 32
+
+
+def gather_from_all(shard, axis, dim):
+    peers = lax.axis_size(axis)
+    repeats = [peers if d == dim else 1 for d in range(shard.ndim)]
+    return lax.all_to_all(
+        jnp.tile(shard, repeats), axis, split_axis=dim, concat_axis=dim, tiled=True
+    )
 
 
 def run_tasks(tasks, first_tiles, second_tiles, contract, count):
@@ -30,7 +38,7 @@
 
 def shards(wave_tiles, left_env, right_env, send_list, left_tasks, right_tasks):
     env_left, env_right = (
-        lax.all_gather(left_env, "sector", axis=1, tiled=True),
+        gather_from_all(left_env, "sector", 1),
         lax.all_gather(right_env, "sector", axis=1, tiled=True),
     )
     env_left = env_left[0]

time: 565 us -> 608 us (1.076)
  waiting for transfers between devices: 286 us -> 316 us
  starting transfers between devices: 11.4 us -> 18.6 us
    all_gather x1 -> x0, waiting for transfers between devices: 102 us -> none  [shards(): lax.all_gather(left_env, 'sector', axis=1, tiled=True)]
    all_to_all x1, waiting for transfers between devices: 90.6 us -> 189 us  [shards(): lax.all_to_all(outgoing, 'sector', split_axis=0, concat_axis=0, tiled=True)]
    all_to_all x0 -> x1, waiting for transfers between devices: none -> 35.4 us  [gather_from_all(): lax.all_to_all(jnp.tile(shard, repeats), axis, split_axis=dim, concat_axi...]
    all_to_all x0 -> x1, starting transfers between devices: none -> 10.8 us  [gather_from_all(): lax.all_to_all(jnp.tile(shard, repeats), axis, split_axis=dim, concat_axi...]
  transfers between devices with their start and end apart: 4 -> 4, of which waited for: 3 -> 3; matrix products, arithmetic and copies ran while one was open for 16% -> 17% of each run, Pallas kernels for 0% -> 0%
where the time goes in v1:
time: 608 us; the launch traced here: 606 us
  waiting for transfers between devices  316 us (52%)
  local copies, waits for them, and re-layouts  115 us (19%)
  other arithmetic  93.9 us (15%)
  matrix products  48.8 us (8%)
  starting transfers between devices  18.6 us (3%)
  between operations  13.5 us (2%)
    all_to_all x1, waiting for transfers between devices, shards(): lax.all_to_all(outgoing, 'sector', split_axis=0, concat_axis=0, tiled=True)  189 us
    psum x1, waiting for transfers between devices, shards(): summed = lax.psum(partial_value, 'term')  90.3 us
    scatter-add x11, other arithmetic, step(): return total.at[rows[:, 2]].add(contract(first, second))  82 us
    gather x11, local copies, waits for them, and re-layouts, step(): first = jnp.take(first_tiles, rows[:, 0], axis=0)  39.8 us
    gather x11, local copies, waits for them, and re-layouts, step(): second = jnp.take(second_tiles, rows[:, 1], axis=0)  38.9 us
    dot_general x8, matrix products, right_product(): jnp.einsum('bvij,bjk->bvik', inter_part, env_part, preferred_element_type...  36.7 us
    all_to_all x1, waiting for transfers between devices, gather_from_all(): lax.all_to_all(jnp.tile(shard, repeats), axis, split_axis=dim, concat_axi...  35.4 us
    transpose x3, local copies, waits for them, and re-layouts, left_product(): jnp.einsum('bij,bvjk->bvik', env_part, wave_part, preferred_element_type=...  16.8 us
  transfers between devices with their start and end apart: 4, of which 3 were waited for; matrix products, arithmetic and copies ran while one was open for 17% of the time, Pallas kernels for 0%

profile of v1, /device:TPU:2, one launch (start us, length us, event | category | flops | bytes accessed | tf_op | source)
XLA Modules:
  0.0 605.8 jit_solution(13523660883666209258)
XLA Ops:
  9.2 10.8 %all-to-all-start.1 = ((bf16[1,64,128,128]{3,2,0,1:T(8,128)(2,1)}), bf16[1,64,128,128]{3,2,0,1:T(8,128)(2,1)S(1)}, u32[]{:S(2)}, u32[]{:S(2)}) async-start(bf16[1,64,128,128]{3,2,0,1:T(8,128)(2,1)} %tile.10), calls=%async_computation.1 | async-start | bytes 4194304 | tf_op jit(solution)/shard_map/all_to_all | solution.py:13
  20.1 6.5 %gather_fusion.4 = bf16[128,2,128,128]{3,2,1,0:T(8,128)(2,1)} fusion(bf16[16,2,128,128]{3,2,1,0:T(8,128)(2,1)S(1)} %copy-done, s32[1024]{0:T(1024)S(1)} %pad_clamp_fusion.4), kind=kCustom, calls=%fused_computation.4 | custom fusion | bytes 16777728 | tf_op jit(solution)/shard_map/jit(_take)/gather | solution.py:48
  26.6 7.5 %select_select_fusion = bf16[128,2,128,128]{3,2,1,0:T(8,128)(2,1)} fusion(bf16[128,2,128,128]{3,2,1,0:T(8,128)(2,1)} %gather_fusion.4, pred[128]{0:T(512)(128)(4,1)S(1)} %get-tuple-element.225, pred[128]{0:T(512)(128)(4,1)S(1)} %get-tuple-element.224), kind=kLoop, calls=%fused_computation.45 | loop fusion | flops 8388608 | bytes 16777472 | tf_op jit(solution)/shard_map/jit(_where)/select_n | solution.py:49
  34.1 35.4 %all-to-all-done.1 = bf16[1,64,128,128]{3,2,0,1:T(8,128)(2,1)S(1)} async-done(((bf16[1,64,128,128]{3,2,0,1:T(8,128)(2,1)}), bf16[1,64,128,128]{3,2,0,1:T(8,128)(2,1)S(1)}, u32[]{:S(2)}, u32[]{:S(2)}) %all-to-all-start.1) | async-done | bytes 2097184 | tf_op jit(solution)/shard_map/all_to_all | solution.py:13
  69.6 7.7 %all-to-all-start = ((bf16[128,2,128,128]{3,2,1,0:T(8,128)(2,1)}), bf16[128,2,128,128]{3,2,1,0:T(8,128)(2,1)}, u32[]{:S(2)}, u32[]{:S(2)}) async-start(bf16[128,2,128,128]{3,2,1,0:T(8,128)(2,1)} %select_select_fusion), calls=%async_computation | async-start | bytes 16777216 | tf_op jit(solution)/shard_map/all_to_all | solution.py:53
  78.1 189.3 %all-to-all-done = bf16[128,2,128,128]{3,2,1,0:T(8,128)(2,1)} async-done(((bf16[128,2,128,128]{3,2,1,0:T(8,128)(2,1)}), bf16[128,2,128,128]{3,2,1,0:T(8,128)(2,1)}, u32[]{:S(2)}, u32[]{:S(2)}) %all-to-all-start) | async-done | bytes 8388640 | tf_op jit(solution)/shard_map/all_to_all | solution.py:53
  269.9 86.2 %while.26 = (s32[]{:T(128)}, f32[32,2,128,128]{3,2,1,0:T(8,128)}, s32[96,3]{0,1:T(4,128)S(1)}, bf16[128,2,128,128]{3,2,1,0:T(8,128)(2,1)}, bf16[64,128,128]{2,1,...) while((s32[]{:T(128)}, f32[32,2,128,128]{3,2,1,0:T(8,128)}, s32[96,3]{0,1:T(4,128)S(1)}, ...), condition=%wide.region_2.4_spmd, body=%wide.region_0.3_spmd.sunk | while | flops 271059520 | bytes 51391044 | solution.py:28
  282.9 5.6 copy.22
  288.6 10.2 %scatter_fusion = f32[32,2,128,128]{3,2,1,0:T(8,128)} fusion(f32[32,2,128,128]{3,2,1,0:T(8,128)} %get-tuple-element.314, s32[32]{0:T(128)S(1)} %get-tuple-element.291, f32[32,2,128,128]{3,2,1,0:T(8,128)} %copy.22), kind=kCustom, calls=%fused_computation.5.clone.1 | custom fusion | flops 1048576 | bytes 12583040 | tf_op jit(solution)/shard_map/while/body/eval_jaxpr/scatter-add | solution.py:26
  311.8 5.6 copy.22
  317.4 10.0 %scatter_fusion = f32[32,2,128,128]{3,2,1,0:T(8,128)} fusion(f32[32,2,128,128]{3,2,1,0:T(8,128)} %get-tuple-element.314, s32[32]{0:T(128)S(1)} %get-tuple-element.291, f32[32,2,128,128]{3,2,1,0:T(8,128)} %copy.22), kind=kCustom, calls=%fused_computation.5.clone.1 | custom fusion | flops 1048576 | bytes 12583040 | tf_op jit(solution)/shard_map/while/body/eval_jaxpr/scatter-add | solution.py:26
  340.5 5.6 copy.22
  346.1 10.0 %scatter_fusion = f32[32,2,128,128]{3,2,1,0:T(8,128)} fusion(f32[32,2,128,128]{3,2,1,0:T(8,128)} %get-tuple-element.314, s32[32]{0:T(128)S(1)} %get-tuple-element.291, f32[32,2,128,128]{3,2,1,0:T(8,128)} %copy.22), kind=kCustom, calls=%fused_computation.5.clone.1 | custom fusion | flops 1048576 | bytes 12583040 | tf_op jit(solution)/shard_map/while/body/eval_jaxpr/scatter-add | solution.py:26
  360.2 145.5 %while.27 = (s32[]{:T(128)}, f32[16,2,128,128]{3,2,1,0:T(8,128)S(1)}, s32[256,3]{0,1:T(4,128)S(1)}, bf16[32,2,128,128]{3,2,1,0:T(8,128)(2,1)}, bf16[64,128,128]{...) while((s32[]{:T(128)}, f32[16,2,128,128]{3,2,1,0:T(8,128)S(1)}, ...), condition=%wide.region_5.7_spmd, body=%wide.region_3.6_spmd.sunk | while | flops 271059520 | bytes 26225168 | solution.py:28
  371.9 6.5 %scatter_fusion.1 = f32[16,2,128,128]{3,2,1,0:T(8,128)S(1)} fusion(f32[16,2,128,128]{3,2,1,0:T(8,128)S(1)} %get-tuple-element.341, s32[32]{0:T(128)S(1)} %get-tuple-element.300, f32[32,2,128,128]{3,2,1,0:T(8,128)} %fusion.34), kind=kCustom, calls=%fused_computation.6.clone.1 | custom fusion | flops 1048576 | bytes 12583040 | tf_op jit(solution)/shard_map/while/body/eval_jaxpr/scatter-add | solution.py:26
  385.5 4.6 fusion.34
  390.1 6.5 %scatter_fusion.1 = f32[16,2,128,128]{3,2,1,0:T(8,128)S(1)} fusion(f32[16,2,128,128]{3,2,1,0:T(8,128)S(1)} %get-tuple-element.341, s32[32]{0:T(128)S(1)} %get-tuple-element.300, f32[32,2,128,128]{3,2,1,0:T(8,128)} %fusion.34), kind=kCustom, calls=%fused_computation.6.clone.1 | custom fusion | flops 1048576 | bytes 12583040 | tf_op jit(solution)/shard_map/while/body/eval_jaxpr/scatter-add | solution.py:26
  408.3 6.5 %scatter_fusion.1 = f32[16,2,128,128]{3,2,1,0:T(8,128)S(1)} fusion(f32[16,2,128,128]{3,2,1,0:T(8,128)S(1)} %get-tuple-element.341, s32[32]{0:T(128)S(1)} %get-tuple-element.300, f32[32,2,128,128]{3,2,1,0:T(8,128)} %fusion.34), kind=kCustom, calls=%fused_computation.6.clone.1 | custom fusion | flops 1048576 | bytes 12583040 | tf_op jit(solution)/shard_map/while/body/eval_jaxpr/scatter-add | solution.py:26
  426.5 6.5 %scatter_fusion.1 = f32[16,2,128,128]{3,2,1,0:T(8,128)S(1)} fusion(f32[16,2,128,128]{3,2,1,0:T(8,128)S(1)} %get-tuple-element.341, s32[32]{0:T(128)S(1)} %get-tuple-element.300, f32[32,2,128,128]{3,2,1,0:T(8,128)} %fusion.34), kind=kCustom, calls=%fused_computation.6.clone.1 | custom fusion | flops 1048576 | bytes 12583040 | tf_op jit(solution)/shard_map/while/body/eval_jaxpr/scatter-add | solution.py:26
  444.7 6.5 %scatter_fusion.1 = f32[16,2,128,128]{3,2,1,0:T(8,128)S(1)} fusion(f32[16,2,128,128]{3,2,1,0:T(8,128)S(1)} %get-tuple-element.341, s32[32]{0:T(128)S(1)} %get-tuple-element.300, f32[32,2,128,128]{3,2,1,0:T(8,128)} %fusion.34), kind=kCustom, calls=%fused_computation.6.clone.1 | custom fusion | flops 1048576 | bytes 12583040 | tf_op jit(solution)/shard_map/while/body/eval_jaxpr/scatter-add | solution.py:26
  462.9 6.5 %scatter_fusion.1 = f32[16,2,128,128]{3,2,1,0:T(8,128)S(1)} fusion(f32[16,2,128,128]{3,2,1,0:T(8,128)S(1)} %get-tuple-element.341, s32[32]{0:T(128)S(1)} %get-tuple-element.300, f32[32,2,128,128]{3,2,1,0:T(8,128)} %fusion.34), kind=kCustom, calls=%fused_computation.6.clone.1 | custom fusion | flops 1048576 | bytes 12583040 | tf_op jit(solution)/shard_map/while/body/eval_jaxpr/scatter-add | solution.py:26
  481.0 6.5 %scatter_fusion.1 = f32[16,2,128,128]{3,2,1,0:T(8,128)S(1)} fusion(f32[16,2,128,128]{3,2,1,0:T(8,128)S(1)} %get-tuple-element.341, s32[32]{0:T(128)S(1)} %get-tuple-element.300, f32[32,2,128,128]{3,2,1,0:T(8,128)} %fusion.34), kind=kCustom, calls=%fused_computation.6.clone.1 | custom fusion | flops 1048576 | bytes 12583040 | tf_op jit(solution)/shard_map/while/body/eval_jaxpr/scatter-add | solution.py:26
  499.2 6.5 %scatter_fusion.1 = f32[16,2,128,128]{3,2,1,0:T(8,128)S(1)} fusion(f32[16,2,128,128]{3,2,1,0:T(8,128)S(1)} %get-tuple-element.341, s32[32]{0:T(128)S(1)} %get-tuple-element.300, f32[32,2,128,128]{3,2,1,0:T(8,128)} %fusion.34), kind=kCustom, calls=%fused_computation.6.clone.1 | custom fusion | flops 1048576 | bytes 12583040 | tf_op jit(solution)/shard_map/while/body/eval_jaxpr/scatter-add | solution.py:26
  507.1 90.3 %all-reduce.2.cloned.1.call-done = f32[16,2,128,128]{3,2,1,0:T(8,128)} async-done(((f32[16,2,128,128]{3,2,1,0:T(8,128)}), f32[16,2,128,128]{3,2,1,0:T(8,128)}) %all-reduce.2.cloned.1.call-update) | async-done | bytes 2097168 | tf_op jit(solution)/shard_map/psum | solution.py:60
  (135 shorter events, 141.0 us)
Async XLA Ops:
  6.5 13.5 %copy-start = (bf16[16,2,128,128]{3,2,1,0:T(8,128)(2,1)S(1)}, bf16[16,2,128,128]{3,2,1,0:T(8,128)(2,1)}, u32[]{:S(2)}) copy-start(bf16[16,2,128,128]{3,2,1,0:T(8,128)(2,1)} %param.12) | copy-start | bytes 3145732
  9.2 10.8 %copy-start.6 = (s32[1,128]{1,0:T(1,128)S(1)}, s32[1,128]{1,0:T(1,128)}, u32[]{:S(2)}) copy-start(s32[1,128]{1,0:T(1,128)} %param.15) | copy-start | bytes 1540
  9.2 60.3 %all-to-all-start.1 = ((bf16[1,64,128,128]{3,2,0,1:T(8,128)(2,1)}), bf16[1,64,128,128]{3,2,0,1:T(8,128)(2,1)S(1)}, u32[]{:S(2)}, u32[]{:S(2)}) async-start(bf16[1,64,128,128]{3,2,0,1:T(8,128)(2,1)} %tile.10), calls=%async_computation.1 | async-start | bytes 4194304 | tf_op jit(solution)/shard_map/all_to_all | solution.py:13
  34.1 44.0 %copy-start.5 = (s32[1,1,96,3]{2,1,3,0:T(1,128)S(1)}, s32[1,1,96,3]{2,1,3,0:T(1,128)}, u32[]{:S(2)}) copy-start(s32[1,1,96,3]{2,1,3,0:T(1,128)} %param.16) | copy-start | bytes 3460
  34.1 44.0 %copy-start.4 = (s32[1,1,256,3]{2,1,3,0:T(1,128)S(1)}, s32[1,1,256,3]{2,1,3,0:T(1,128)}, u32[]{:S(2)}) copy-start(s32[1,1,256,3]{2,1,3,0:T(1,128)} %param.17) | copy-start | bytes 9220
  69.6 197.9 %all-to-all-start = ((bf16[128,2,128,128]{3,2,1,0:T(8,128)(2,1)}), bf16[128,2,128,128]{3,2,1,0:T(8,128)(2,1)}, u32[]{:S(2)}, u32[]{:S(2)}) async-start(bf16[128,2,128,128]{3,2,1,0:T(8,128)(2,1)} %select_select_fusion), calls=%async_computation | async-start | bytes 16777216 | tf_op jit(solution)/shard_map/all_to_all | solution.py:53
  77.3 282.7 %all-gather.2.cloned.1.call-start = ((), (), s32[]{:S(2)}) async-start(), calls=%async_computation.2 | async-start | bytes 2129920 | tf_op jit(solution)/shard_map/all_gather | solution.py:42
  78.0 519.3 %all-reduce.2.cloned.1.call-start = ((), (), s32[]{:S(2)}) async-start(), calls=%async_computation.3 | async-start | bytes 4194304 | tf_op jit(solution)/shard_map/psum | solution.py:60
  269.9 1.3 copy-start.2
  288.6 10.2 %copy-start.3 = (bf16[64,128,128]{2,1,0:T(8,128)(2,1)S(1)}, bf16[64,128,128]{2,1,0:T(8,128)(2,1)}, u32[]{:S(2)}) copy-start(bf16[64,128,128]{2,1,0:T(8,128)(2,1)} %copy-done.2) | copy-start | bytes 6291460 | tf_op jit(solution)/shard_map/while
  298.7 1.3 copy-start.2
  317.4 10.0 %copy-start.3 = (bf16[64,128,128]{2,1,0:T(8,128)(2,1)S(1)}, bf16[64,128,128]{2,1,0:T(8,128)(2,1)}, u32[]{:S(2)}) copy-start(bf16[64,128,128]{2,1,0:T(8,128)(2,1)} %copy-done.2) | copy-start | bytes 6291460 | tf_op jit(solution)/shard_map/while
  327.4 1.3 copy-start.2
  346.1 10.0 %copy-start.3 = (bf16[64,128,128]{2,1,0:T(8,128)(2,1)S(1)}, bf16[64,128,128]{2,1,0:T(8,128)(2,1)}, u32[]{:S(2)}) copy-start(bf16[64,128,128]{2,1,0:T(8,128)(2,1)} %copy-done.2) | copy-start | bytes 6291460 | tf_op jit(solution)/shard_map/while
  505.7 1.3 copy-start.1
Sparse Core Ops, SparseCore 0:
  81.5 99.7 all-gather.1
  507.2 90.0 all-reduce.1
